TPU v7x, 128 devices: a whole 4x4x4 slice. The times are simulated.
128 devices in a mesh: grp: 4 (over z_lo, core), mem: 32 (over z_hi, x, y).
Axes of the slice: x: 4, y: 4, z: 4 (z_hi: 2, z_lo: 2; z = z_hi * 2 + z_lo), core: 2. Of those that a mesh axis runs over, the one named last changes fastest.
Arguments:
- source_pts: float32 [64, 32768], P(None, ('grp', 'mem')), may hold values from -30 to 30
- target_pts: float32 [64, 32768], P(None, ('grp', 'mem')), may hold values from -30 to 30
- source_pot: float32 [32768], P(('grp', 'mem')), may hold values from -8 to 520
- target_pot: float32 [32768], P(('grp', 'mem')), may hold values from -8 to 520
- source_logw: float32 [32768], P(('grp', 'mem')), may hold values from -1 to 4
- target_logw: float32 [32768], P(('grp', 'mem')), may hold values from -1 to 4
Outputs:
- source_new: float32 [32768], P(('grp', 'mem'))
- target_new: float32 [32768], P(('grp', 'mem'))
All inputs are finite; a program needn't handle non-finite values.
Results may differ from a plain program's by a relative error of at most 0.0001.
Values sent between devices are 32-bit elements; how exact they have to be, the bound alone decides.
No kernel may reach another device: no remote copies, remote signals or barrier semaphores. Data moves between devices by JAX's collectives and lax.ppermute only.
A program may use at most 64 MiB of HBM per device.

v0:
```python
import math
import jax
import jax.numpy as jnp
from jax import lax
from jax.sharding import Mesh
from jax.sharding import PartitionSpec as P

GRP_MEM = ("grp_0", "grp_1", "mem_0", "mem_1", "mem_2")
MEM = ("mem_0", "mem_1", "mem_2")
GRP = ("grp_0", "grp_1")
epsilon = 4.0
floor_value = -1e30


def by_axis(x, axes):
    for axis in axes:
        x = lax.pmax(x, axis)
    return x


def by_axis_2(x, axes):
    for axis in axes:
        x = lax.psum(x, axis)
    return x


def in_order(pieces, dim):
    dims = list(pieces.shape[1:])
    dims[dim] *= pieces.shape[0]
    return jnp.moveaxis(pieces, 0, dim).reshape(dims)


def sent_to_all(x, axis):
    copies = jnp.broadcast_to(x, (lax.axis_size(axis), *x.shape))
    return lax.all_to_all(copies, axis, split_axis=0, concat_axis=0, tiled=True)


def collect(x, axis, dim):
    return in_order(sent_to_all(x, axis), dim)


def over_copies(x, axis):
    return sent_to_all(x, axis).max(axis=0)


def cut_along(x, dim, devices):
    dims = x.shape
    pieces = x.reshape(*dims[:dim], devices, dims[dim] // devices, *dims[dim + 1 :])
    return jnp.moveaxis(pieces, dim, 0)


def sum_at_owner(x, axis, dim):
    devices = lax.axis_size(axis)
    pieces = lax.all_to_all(cut_along(x, dim, devices), axis, 0, 0, tiled=True)
    return jnp.sum(pieces, axis=0)


def sweep(carry, points, squares, row_term, moving, offset):
    count = moving.shape[1]
    limit = 128
    width = math.gcd(count, limit)

    def block(index, state):
        row_max, row_sum, col_max, col_sum = state
        begin = index * width
        cols = lax.dynamic_slice_in_dim(moving, begin, width, 1)
        ycols = cols[:-1]
        cvals = cols[-1]
        ysq = 0.5 * jnp.sum(ycols * ycols, 0)
        cross = lax.dot_general(
            points,
            ycols,
            (((0,), (0,)), ((), ())),
            precision=lax.Precision.HIGHEST,
            preferred_element_type=jnp.float32,
        )
        half = (squares[:, None] + ysq[None, :] - cross) / epsilon
        scores = cvals[None, :] - half
        new_row = jnp.maximum(row_max, jnp.max(scores, 1))
        row_sum = row_sum * jnp.exp(row_max - new_row) + jnp.sum(
            jnp.exp(scores - new_row[:, None]), 1
        )
        others = row_term[:, None] - half
        place = offset + begin
        old_max = lax.dynamic_slice_in_dim(col_max, place, width, 0)
        old_sum = lax.dynamic_slice_in_dim(col_sum, place, width, 0)
        new_col = jnp.maximum(old_max, jnp.max(others, 0))
        new_sum = old_sum * jnp.exp(old_max - new_col) + jnp.sum(
            jnp.exp(others - new_col[None, :]), 0
        )
        col_max = lax.dynamic_update_slice_in_dim(col_max, new_col, place, 0)
        col_sum = lax.dynamic_update_slice_in_dim(col_sum, new_sum, place, 0)
        return (new_row, row_sum, col_max, col_sum)

    return lax.fori_loop(0, count // width, block, carry)


def totals(source_logw, target_logw):
    peaks = (by_axis(jnp.max(source_logw), GRP_MEM), by_axis(jnp.max(target_logw), GRP_MEM))
    masses = (
        by_axis_2(jnp.sum(jnp.exp(source_logw - peaks[0])), GRP_MEM),
        by_axis_2(jnp.sum(jnp.exp(target_logw - peaks[1])), GRP_MEM),
    )
    return (peaks[0] + jnp.log(masses[0]), peaks[1] + jnp.log(masses[1]))


def local(source_pts, target_pts, source_pot, target_pot, source_logw, target_logw):
    members = lax.axis_size(MEM)
    rows = source_pts.shape[1]
    outer = rows * members
    row_term = source_logw + source_pot / epsilon
    col_term = target_logw + target_pot / epsilon
    moving = jnp.concatenate([target_pts, col_term[None, :]], 0)
    standing = jnp.concatenate([source_pts, row_term[None, :]], 0)
    row_block = collect(standing, MEM, 1)
    col_block = collect(moving, GRP, 1)
    block_pts = row_block[:-1]
    block_terms = row_block[-1]
    block_sq = 0.5 * jnp.sum(block_pts * block_pts, 0)
    span = col_block.shape[1]
    carry = (
        jnp.full((outer,), floor_value, jnp.float32),
        jnp.zeros((outer,), jnp.float32),
        jnp.full((span,), floor_value, jnp.float32),
        jnp.zeros((span,), jnp.float32),
    )
    row_max, row_sum, col_max, col_sum = sweep(
        carry, block_pts, block_sq, block_terms, col_block, 0
    )
    rpeak = over_copies(row_max, MEM)
    own_rsum = sum_at_owner(row_sum * jnp.exp(row_max - rpeak), MEM, 0)
    own_rmax = lax.dynamic_slice_in_dim(rpeak, lax.axis_index(MEM) * rows, rows, 0)
    row_total = own_rmax + jnp.log(own_rsum)
    cpeak = over_copies(col_max, GRP)
    own_sum = sum_at_owner(col_sum * jnp.exp(col_max - cpeak), GRP, 0)
    own_max = lax.dynamic_slice_in_dim(cpeak, lax.axis_index(GRP) * rows, rows, 0)
    col_total = own_max + jnp.log(own_sum)
    src_norm, tgt_norm = totals(source_logw, target_logw)
    row_hat = -epsilon * (row_total - tgt_norm)
    col_hat = -epsilon * (col_total - src_norm)
    return (0.5 * (source_pot + row_hat), 0.5 * (target_pot + col_hat))


def solution(mesh):
    finer = Mesh(mesh.devices.reshape(2, 2, 2, 4, 4), ("grp_0", "grp_1", "mem_0", "mem_1", "mem_2"))
    return jax.shard_map(
        local,
        mesh=finer,
        in_specs=(
            P(None, GRP_MEM),
            P(None, GRP_MEM),
            P(GRP_MEM),
            P(GRP_MEM),
            P(GRP_MEM),
            P(GRP_MEM),
        ),
        out_specs=(P(GRP_MEM), P(GRP_MEM)),
        check_vma=False,
    )
```

profile of v0, /device:TPU:0, one launch (start us, length us, event | category | flops | bytes accessed | tf_op | source)
XLA Modules:
  0.0 235.5 jit_solution(10569163708637977095)
XLA Ops:
  3.2 5.6 %all-reduce.9 = (f32[]{:T(128)}, f32[]{:T(128)}) all-reduce(f32[]{:T(128)} %reduce_max.63, f32[]{:T(128)} %reduce_max.65), channel_id=1, replica_groups=mesh['grp_0'=2,'grp_1'=2,'mem_0'=2,'mem_1'=4,'mem_2'=4] {'grp_0'}, use_global_device_ids=true, to_apply=%region_11.0 | all-reduce | flops 2 | bytes 16 | tf_op jit(solution)/shard_map/pmax | solution.py:17
  8.8 3.1 %all-reduce.8 = (f32[]{:T(128)}, f32[]{:T(128)}) all-reduce(f32[]{:T(128)} %get-tuple-element.233, f32[]{:T(128)} %get-tuple-element.234), channel_id=1, replica_groups=mesh['grp_0'=2,'grp_1'=2,'mem_0'=2,'mem_1'=4,'mem_2'=4] {'grp_1'}, use_global_device_ids=true, to_apply=%region_12.0 | all-reduce | flops 2 | bytes 16 | tf_op jit(solution)/shard_map/pmax | solution.py:17
  11.8 7.5 %all-reduce.7 = (f32[]{:T(128)}, f32[]{:T(128)}) all-reduce(f32[]{:T(128)} %get-tuple-element.231, f32[]{:T(128)} %get-tuple-element.232), channel_id=1, replica_groups=mesh['grp_0'=2,'grp_1'=2,'mem_0'=2,'mem_1'=4,'mem_2'=4] {'mem_0'}, use_global_device_ids=true, to_apply=%region_13.0 | all-reduce | flops 2 | bytes 16 | tf_op jit(solution)/shard_map/pmax | solution.py:17
  19.3 11.1 %all-reduce.3 = (f32[]{:T(128)}, f32[]{:T(128)}) all-reduce(f32[]{:T(128)} %get-tuple-element.229, f32[]{:T(128)} %get-tuple-element.230), channel_id=1, replica_groups=mesh['grp_0'=2,'grp_1'=2,'mem_0'=2,'mem_1'=4,'mem_2'=4] {'mem_1'}, use_global_device_ids=true, to_apply=%region_14.0 | all-reduce | flops 2 | bytes 16 | tf_op jit(solution)/shard_map/pmax | solution.py:17
  30.4 11.4 %all-reduce.2 = (f32[]{:T(128)}, f32[]{:T(128)}) all-reduce(f32[]{:T(128)} %get-tuple-element.221, f32[]{:T(128)} %get-tuple-element.222), channel_id=1, replica_groups=mesh['grp_0'=2,'grp_1'=2,'mem_0'=2,'mem_1'=4,'mem_2'=4] {'mem_2'}, use_global_device_ids=true, to_apply=%region_15.0 | all-reduce | flops 2 | bytes 16 | tf_op jit(solution)/shard_map/pmax | solution.py:17
  41.8 2.6 %exponential_reduce_fusion.2 = (f32[]{:T(128)}, f32[256]{0:T(256)S(1)}, f32[256]{0:T(256)S(1)}, f32[]{:T(128)}) fusion(f32[256]{0:T(256)} %param.12, f32[]{:T(128)} %get-tuple-element.220, f32[256]{0:T(256)} %param.10, f32[256]{0:T(256)} %param.13, f32[256]{0:T(256)} %param.11, f32[]{:T(128)} %get-tuple-element.219), kind=kLoop, calls=%fused_computation.25 | loop fusion | flops 2046 | bytes 6160 | tf_op jit(solution)/shard_map/reduce_sum | solution.py:101
  46.0 3.5 %all-to-all-start = ((f32[4,65,256]{2,1,0:T(8,128)}), f32[4,65,256]{2,1,0:T(8,128)S(1)}, u32[]{:S(2)}, u32[]{:S(2)}) async-start(f32[4,65,256]{2,1,0:T(8,128)} %broadcast_in_dim.47), calls=%async_computation | async-start | bytes 589824 | tf_op jit(solution)/shard_map/all_to_all | solution.py:35
  50.3 5.5 %all-to-all-done = f32[4,65,256]{2,1,0:T(8,128)S(1)} async-done(((f32[4,65,256]{2,1,0:T(8,128)}), f32[4,65,256]{2,1,0:T(8,128)S(1)}, u32[]{:S(2)}, u32[]{:S(2)}) %all-to-all-start) | async-done | bytes 266272 | tf_op jit(solution)/shard_map/all_to_all | solution.py:35
  57.3 5.8 %all-to-all-start.1 = ((f32[32,65,256]{2,1,0:T(8,128)}), f32[32,65,256]{2,1,0:T(8,128)S(1)}, u32[]{:S(2)}, u32[]{:S(2)}) async-start(f32[32,65,256]{2,1,0:T(8,128)} %broadcast_in_dim.49), calls=%async_computation.1 | async-start | bytes 4718592 | tf_op jit(solution)/shard_map/all_to_all | solution.py:35
  63.4 31.0 %all-to-all-done.1 = f32[32,65,256]{2,1,0:T(8,128)S(1)} async-done(((f32[32,65,256]{2,1,0:T(8,128)}), f32[32,65,256]{2,1,0:T(8,128)S(1)}, u32[]{:S(2)}, u32[]{:S(2)}) %all-to-all-start.1) | async-done | bytes 2129952 | tf_op jit(solution)/shard_map/all_to_all | solution.py:35
  95.1 53.8 %while.20 = (s32[]{:T(128)}, f32[8192]{0:T(1024)S(1)}, f32[8192]{0:T(1024)S(1)}, f32[1024]{0:T(1024)S(1)}, f32[1024]{0:T(1024)S(1)}, /*index=5*/f32[65,1024]{1,0...) while((s32[]{:T(128)}, f32[8192]{0:T(1024)S(1)}, ...), condition=%wide.region_7.0_spmd.clone, body=%wide.region_1.0_spmd.clone.sunk | while | flops 818995456 | bytes 11102442 | solution.py:95
  95.2 4.5 %subtract_reduce_fusion.3 = (f32[128]{0:T(128)S(1)}, f32[8192]{0:T(1024)S(1)}, f32[8192,128]{0,1:T(8,128)S(1)}) fusion(f32[8192]{0:T(1024)S(1)} %bitcast.36, f32[128]{0:T(128)S(1)} %dynamic-slice_bitcast_fusion.2, f32[64,8192]{1,0:T(8,128)S(1)} %get-tuple-element.350, f32[65,1024]{1,0:T(8,128)S(1)} %get-tuple-element.348, s32[]{:T(128)S(6)} %select_n.21, ...), kind=kOutput, calls=%fused_computation.5.clone.1 | convolution fusion | flops 812638080 | bytes 6424068 | tf_op jit(solution)/shard_map/while/body/eval_jaxpr/dot_general | solution.py:70
  101.9 4.5 %subtract_reduce_fusion.3 = (f32[128]{0:T(128)S(1)}, f32[8192]{0:T(1024)S(1)}, f32[8192,128]{0,1:T(8,128)S(1)}) fusion(f32[8192]{0:T(1024)S(1)} %bitcast.36, f32[128]{0:T(128)S(1)} %dynamic-slice_bitcast_fusion.2, f32[64,8192]{1,0:T(8,128)S(1)} %get-tuple-element.350, f32[65,1024]{1,0:T(8,128)S(1)} %get-tuple-element.348, s32[]{:T(128)S(6)} %select_n.21, ...), kind=kOutput, calls=%fused_computation.5.clone.1 | convolution fusion | flops 812638080 | bytes 6424068 | tf_op jit(solution)/shard_map/while/body/eval_jaxpr/dot_general | solution.py:70
  108.6 4.5 %subtract_reduce_fusion.3 = (f32[128]{0:T(128)S(1)}, f32[8192]{0:T(1024)S(1)}, f32[8192,128]{0,1:T(8,128)S(1)}) fusion(f32[8192]{0:T(1024)S(1)} %bitcast.36, f32[128]{0:T(128)S(1)} %dynamic-slice_bitcast_fusion.2, f32[64,8192]{1,0:T(8,128)S(1)} %get-tuple-element.350, f32[65,1024]{1,0:T(8,128)S(1)} %get-tuple-element.348, s32[]{:T(128)S(6)} %select_n.21, ...), kind=kOutput, calls=%fused_computation.5.clone.1 | convolution fusion | flops 812638080 | bytes 6424068 | tf_op jit(solution)/shard_map/while/body/eval_jaxpr/dot_general | solution.py:70
  115.3 4.5 %subtract_reduce_fusion.3 = (f32[128]{0:T(128)S(1)}, f32[8192]{0:T(1024)S(1)}, f32[8192,128]{0,1:T(8,128)S(1)}) fusion(f32[8192]{0:T(1024)S(1)} %bitcast.36, f32[128]{0:T(128)S(1)} %dynamic-slice_bitcast_fusion.2, f32[64,8192]{1,0:T(8,128)S(1)} %get-tuple-element.350, f32[65,1024]{1,0:T(8,128)S(1)} %get-tuple-element.348, s32[]{:T(128)S(6)} %select_n.21, ...), kind=kOutput, calls=%fused_computation.5.clone.1 | convolution fusion | flops 812638080 | bytes 6424068 | tf_op jit(solution)/shard_map/while/body/eval_jaxpr/dot_general | solution.py:70
  120.1 1.7 exponential_reduce_fusion.5
  122.1 4.5 %subtract_reduce_fusion.3 = (f32[128]{0:T(128)S(1)}, f32[8192]{0:T(1024)S(1)}, f32[8192,128]{0,1:T(8,128)S(1)}) fusion(f32[8192]{0:T(1024)S(1)} %bitcast.36, f32[128]{0:T(128)S(1)} %dynamic-slice_bitcast_fusion.2, f32[64,8192]{1,0:T(8,128)S(1)} %get-tuple-element.350, f32[65,1024]{1,0:T(8,128)S(1)} %get-tuple-element.348, s32[]{:T(128)S(6)} %select_n.21, ...), kind=kOutput, calls=%fused_computation.5.clone.1 | convolution fusion | flops 812638080 | bytes 6424068 | tf_op jit(solution)/shard_map/while/body/eval_jaxpr/dot_general | solution.py:70
  128.8 4.5 %subtract_reduce_fusion.3 = (f32[128]{0:T(128)S(1)}, f32[8192]{0:T(1024)S(1)}, f32[8192,128]{0,1:T(8,128)S(1)}) fusion(f32[8192]{0:T(1024)S(1)} %bitcast.36, f32[128]{0:T(128)S(1)} %dynamic-slice_bitcast_fusion.2, f32[64,8192]{1,0:T(8,128)S(1)} %get-tuple-element.350, f32[65,1024]{1,0:T(8,128)S(1)} %get-tuple-element.348, s32[]{:T(128)S(6)} %select_n.21, ...), kind=kOutput, calls=%fused_computation.5.clone.1 | convolution fusion | flops 812638080 | bytes 6424068 | tf_op jit(solution)/shard_map/while/body/eval_jaxpr/dot_general | solution.py:70
  135.5 4.5 %subtract_reduce_fusion.3 = (f32[128]{0:T(128)S(1)}, f32[8192]{0:T(1024)S(1)}, f32[8192,128]{0,1:T(8,128)S(1)}) fusion(f32[8192]{0:T(1024)S(1)} %bitcast.36, f32[128]{0:T(128)S(1)} %dynamic-slice_bitcast_fusion.2, f32[64,8192]{1,0:T(8,128)S(1)} %get-tuple-element.350, f32[65,1024]{1,0:T(8,128)S(1)} %get-tuple-element.348, s32[]{:T(128)S(6)} %select_n.21, ...), kind=kOutput, calls=%fused_computation.5.clone.1 | convolution fusion | flops 812638080 | bytes 6424068 | tf_op jit(solution)/shard_map/while/body/eval_jaxpr/dot_general | solution.py:70
  140.3 1.7 exponential_reduce_fusion.5
  142.2 4.5 %subtract_reduce_fusion.3 = (f32[128]{0:T(128)S(1)}, f32[8192]{0:T(1024)S(1)}, f32[8192,128]{0,1:T(8,128)S(1)}) fusion(f32[8192]{0:T(1024)S(1)} %bitcast.36, f32[128]{0:T(128)S(1)} %dynamic-slice_bitcast_fusion.2, f32[64,8192]{1,0:T(8,128)S(1)} %get-tuple-element.350, f32[65,1024]{1,0:T(8,128)S(1)} %get-tuple-element.348, s32[]{:T(128)S(6)} %select_n.21, ...), kind=kOutput, calls=%fused_computation.5.clone.1 | convolution fusion | flops 812638080 | bytes 6424068 | tf_op jit(solution)/shard_map/while/body/eval_jaxpr/dot_general | solution.py:70
  148.9 6.2 %all_to_all.40 = f32[4,1,1024]{2,1,0:T(1,128)S(1)} all-to-all(f32[4,1,1024]{2,1,0:T(1,128)S(1)} %broadcast_in_dim.51), channel_id=1, replica_groups=mesh['grp_0'=2,'grp_1'=2,'mem_0'=2,'mem_1'=4,'mem_2'=4] {'grp_0','grp_1'}, dimensions={0} | all-to-all | bytes 32768 | tf_op jit(solution)/shard_map/all_to_all | solution.py:35
  155.2 6.1 %all_to_all.41 = f32[4,1,256]{2,1,0:T(1,128)S(1)} all-to-all(f32[4,1,256]{2,1,0:T(1,128)S(1)} %bitcast.42), channel_id=1, replica_groups=mesh['grp_0'=2,'grp_1'=2,'mem_0'=2,'mem_1'=4,'mem_2'=4] {'grp_0','grp_1'}, dimensions={0} | all-to-all | bytes 8192 | tf_op jit(solution)/shard_map/all_to_all | solution.py:54
  161.3 1.9 broadcast_in_dim.50
  163.2 7.4 %all-to-all-start.2 = ((f32[32,1,8192]{2,1,0:T(1,128)}), f32[32,1,8192]{2,1,0:T(1,128)S(1)}, u32[]{:S(2)}, u32[]{:S(2)}) async-start(f32[32,1,8192]{2,1,0:T(1,128)} %broadcast_in_dim.50), calls=%async_computation.2 | async-start | bytes 2097152 | tf_op jit(solution)/shard_map/all_to_all | solution.py:35
  170.7 5.5 %all-reduce.6 = (f32[]{:T(128)}, f32[]{:T(128)}) all-reduce(f32[]{:T(128)} %get-tuple-element.245, f32[]{:T(128)} %get-tuple-element.240), channel_id=1, replica_groups=mesh['grp_0'=2,'grp_1'=2,'mem_0'=2,'mem_1'=4,'mem_2'=4] {'grp_0'}, use_global_device_ids=true, to_apply=%region_17.0 | all-reduce | flops 2 | bytes 16 | tf_op jit(solution)/shard_map/psum | solution.py:23
  176.2 3.1 %all-reduce.5 = (f32[]{:T(128)}, f32[]{:T(128)}) all-reduce(f32[]{:T(128)} %get-tuple-element.227, f32[]{:T(128)} %get-tuple-element.228), channel_id=1, replica_groups=mesh['grp_0'=2,'grp_1'=2,'mem_0'=2,'mem_1'=4,'mem_2'=4] {'grp_1'}, use_global_device_ids=true, to_apply=%region_18.0 | all-reduce | flops 2 | bytes 16 | tf_op jit(solution)/shard_map/psum | solution.py:23
  179.3 7.3 %all-reduce.4 = (f32[]{:T(128)}, f32[]{:T(128)}) all-reduce(f32[]{:T(128)} %get-tuple-element.225, f32[]{:T(128)} %get-tuple-element.226), channel_id=1, replica_groups=mesh['grp_0'=2,'grp_1'=2,'mem_0'=2,'mem_1'=4,'mem_2'=4] {'mem_0'}, use_global_device_ids=true, to_apply=%region_19.0 | all-reduce | flops 2 | bytes 16 | tf_op jit(solution)/shard_map/psum | solution.py:23
  186.6 15.7 %all-reduce.1 = (f32[]{:T(128)}, f32[]{:T(128)}) all-reduce(f32[]{:T(128)} %get-tuple-element.223, f32[]{:T(128)} %get-tuple-element.224), channel_id=1, replica_groups=mesh['grp_0'=2,'grp_1'=2,'mem_0'=2,'mem_1'=4,'mem_2'=4] {'mem_1'}, use_global_device_ids=true, to_apply=%region_20.0 | all-reduce | flops 2 | bytes 16 | tf_op jit(solution)/shard_map/psum | solution.py:23
  202.3 12.9 %all-reduce = (f32[]{:T(128)}, f32[]{:T(128)}) all-reduce(f32[]{:T(128)} %get-tuple-element.217, f32[]{:T(128)} %get-tuple-element.218), channel_id=1, replica_groups=mesh['grp_0'=2,'grp_1'=2,'mem_0'=2,'mem_1'=4,'mem_2'=4] {'mem_2'}, use_global_device_ids=true, to_apply=%region_21.0 | all-reduce | flops 2 | bytes 16 | tf_op jit(solution)/shard_map/psum | solution.py:23
  219.1 5.8 %all-to-all-start.3 = ((f32[32,1,256]{2,1,0:T(1,128)}), f32[32,1,256]{2,1,0:T(1,128)S(1)}, u32[]{:S(2)}, u32[]{:S(2)}) async-start(f32[32,1,256]{2,1,0:T(1,128)} %bitcast.5), calls=%async_computation.3 | async-start | bytes 65536 | tf_op jit(solution)/shard_map/all_to_all | solution.py:54
  225.6 9.2 %all-to-all-done.3 = f32[32,1,256]{2,1,0:T(1,128)S(1)} async-done(((f32[32,1,256]{2,1,0:T(1,128)}), f32[32,1,256]{2,1,0:T(1,128)S(1)}, u32[]{:S(2)}, u32[]{:S(2)}) %all-to-all-start.3) | async-done | bytes 32800 | tf_op jit(solution)/shard_map/all_to_all | solution.py:54
  (118 shorter events, 23.9 us)
Async XLA Ops:
  46.0 9.8 %all-to-all-start = ((f32[4,65,256]{2,1,0:T(8,128)}), f32[4,65,256]{2,1,0:T(8,128)S(1)}, u32[]{:S(2)}, u32[]{:S(2)}) async-start(f32[4,65,256]{2,1,0:T(8,128)} %broadcast_in_dim.47), calls=%async_computation | async-start | bytes 589824 | tf_op jit(solution)/shard_map/all_to_all | solution.py:35
  57.3 37.1 %all-to-all-start.1 = ((f32[32,65,256]{2,1,0:T(8,128)}), f32[32,65,256]{2,1,0:T(8,128)S(1)}, u32[]{:S(2)}, u32[]{:S(2)}) async-start(f32[32,65,256]{2,1,0:T(8,128)} %broadcast_in_dim.49), calls=%async_computation.1 | async-start | bytes 4718592 | tf_op jit(solution)/shard_map/all_to_all | solution.py:35
  148.9 76.0 %copy-start = (f32[256]{0:T(256)S(1)}, f32[256]{0:T(256)}, u32[]{:S(2)}) copy-start(f32[256]{0:T(256)} %param.11) | copy-start | bytes 3076
  148.9 85.9 %copy-start.1 = (f32[256]{0:T(256)S(1)}, f32[256]{0:T(256)}, u32[]{:S(2)}) copy-start(f32[256]{0:T(256)} %param.10) | copy-start | bytes 3076
  163.2 54.6 %all-to-all-start.2 = ((f32[32,1,8192]{2,1,0:T(1,128)}), f32[32,1,8192]{2,1,0:T(1,128)S(1)}, u32[]{:S(2)}, u32[]{:S(2)}) async-start(f32[32,1,8192]{2,1,0:T(1,128)} %broadcast_in_dim.50), calls=%async_computation.2 | async-start | bytes 2097152 | tf_op jit(solution)/shard_map/all_to_all | solution.py:35
  219.1 15.6 %all-to-all-start.3 = ((f32[32,1,256]{2,1,0:T(1,128)}), f32[32,1,256]{2,1,0:T(1,128)S(1)}, u32[]{:S(2)}, u32[]{:S(2)}) async-start(f32[32,1,256]{2,1,0:T(1,128)} %bitcast.5), calls=%async_computation.3 | async-start | bytes 65536 | tf_op jit(solution)/shard_map/all_to_all | solution.py:54
where the time goes:
time: 236 us; the launch traced here: 235 us
  blocking collectives  95.3 us (40%)
  waiting for transfers between devices  45.7 us (19%)
  matrix products  36.4 us (15%)
  other arithmetic  27.1 us (11%)
  starting transfers between devices  22.5 us (10%)
  local copies, waits for them, and re-layouts  4.76 us (2%)
  between operations  3.45 us (1%)
    psum x5, blocking collectives, by_axis_2(): x = lax.psum(x, axis)  44.4 us
    pmax x5, blocking collectives, by_axis(): x = lax.pmax(x, axis)  38.6 us
    all_to_all x3, waiting for transfers between devices, sent_to_all(): return lax.all_to_all(copies, axis, split_axis=0, concat_axis=0, tiled=True)  36.5 us
    dot_general x8, matrix products, block(): lax.dot_general(points, ycols, (((0,), (0,)), ((), ())), precision=lax.Pr...  36.4 us
    all_to_all x3, starting transfers between devices, sent_to_all(): return lax.all_to_all(copies, axis, split_axis=0, concat_axis=0, tiled=True)  16.7 us
    reduce_sum x8, other arithmetic, block(): jnp.sum(jnp.exp(others - new_col[None, :]), 0)  13.5 us
    all_to_all x1, waiting for transfers between devices, sum_at_owner(): pieces = lax.all_to_all(cut_along(x, dim, devices), axis, 0, 0, tiled=True)  9.15 us
    all_to_all x1, blocking collectives, sent_to_all(): return lax.all_to_all(copies, axis, split_axis=0, concat_axis=0, tiled=True)  6.21 us
  transfers between devices with their start and end apart: 4, of which 3 were waited for; matrix products, arithmetic and copies ran while one was open for 1% of the time, Pallas kernels for 0%

commit v1 on v0

--- a/solution.py
+++ b/solution.py
@@ -20,7 +20,7 @@
 
 def by_axis_2(x, axes):
     for axis in axes:
-        x = lax.psum(x, axis)
+        x = jnp.sum(lax.all_gather(x, axis), axis=0)
     return x
 
 

time: 236 us -> 282 us (1.19)
  other arithmetic: 27.1 us -> 50.3 us
  local copies, waits for them, and re-layouts: 4.76 us -> 22.1 us
  matrix products: 36.4 us -> 47.8 us
  blocking collectives: 95.3 us -> 88.7 us
    psum x5 -> x0, blocking collectives: 44.4 us -> none  [by_axis_2(): x = lax.psum(x, axis)]
    unnamed x0 -> x5, blocking collectives: none -> 37.8 us
    unnamed x7 -> x42, local copies, waits for them, and re-layouts: 0.13 us -> 17.4 us
    reduce_sum x8, other arithmetic: 13.5 us -> 30.6 us  [block(): jnp.sum(jnp.exp(others - new_col[None, :]), 0)]
    dot_general x8, matrix products: 36.4 us -> 47.8 us  [block(): lax.dot_general(points, ycols, (((0,), (0,)), ((), ())), precision=lax.Pr...]
    reduce_sum x0 -> x10, other arithmetic: none -> 6 us  [by_axis_2(): x = jnp.sum(lax.all_gather(x, axis), axis=0)]
  transfers between devices with their start and end apart: 4 -> 4, of which waited for: 3 -> 3; matrix products, arithmetic and copies ran while one was open for 1% -> 9% of each run, Pallas kernels for 0% -> 0%
where the time goes in v1:
time: 282 us; the launch traced here: 281 us
  blocking collectives  88.7 us (31%)
  other arithmetic  50.3 us (18%)
  matrix products  47.8 us (17%)
  waiting for transfers between devices  45.7 us (16%)
  starting transfers between devices  22.5 us (8%)
  local copies, waits for them, and re-layouts  22.1 us (8%)
  between operations  3.57 us (1%)
    dot_general x8, matrix products, block(): lax.dot_general(points, ycols, (((0,), (0,)), ((), ())), precision=lax.Pr...  47.8 us
    pmax x5, blocking collectives, by_axis(): x = lax.pmax(x, axis)  38.6 us
    unnamed x5, blocking collectives  37.8 us
    all_to_all x3, waiting for transfers between devices, sent_to_all(): return lax.all_to_all(copies, axis, split_axis=0, concat_axis=0, tiled=True)  36.5 us
    reduce_sum x8, other arithmetic, block(): jnp.sum(jnp.exp(others - new_col[None, :]), 0)  30.6 us
    unnamed x42, local copies, waits for them, and re-layouts  17.4 us
    all_to_all x3, starting transfers between devices, sent_to_all(): return lax.all_to_all(copies, axis, split_axis=0, concat_axis=0, tiled=True)  16.7 us
    all_to_all x1, waiting for transfers between devices, sum_at_owner(): pieces = lax.all_to_all(cut_along(x, dim, devices), axis, 0, 0, tiled=True)  9.15 us
  transfers between devices with their start and end apart: 4, of which 3 were waited for; matrix products, arithmetic and copies ran while one was open for 9% of the time, Pallas kernels for 0%

profile of v1, /device:TPU:0, one launch (start us, length us, event | category | flops | bytes accessed | tf_op | source)
XLA Modules:
  0.0 281.1 jit_solution(5034064486585965825)
XLA Ops:
  3.2 5.6 %all-reduce.19 = (f32[]{:T(128)}, f32[]{:T(128)}) all-reduce(f32[]{:T(128)} %reduce_max.63, f32[]{:T(128)} %reduce_max.65), channel_id=1, replica_groups=mesh['grp_0'=2,'grp_1'=2,'mem_0'=2,'mem_1'=4,'mem_2'=4] {'grp_0'}, use_global_device_ids=true, to_apply=%region_11.0 | all-reduce | flops 2 | bytes 16 | tf_op jit(solution)/shard_map/pmax | solution.py:17
  11.8 7.5 %all-reduce.17 = (f32[]{:T(128)}, f32[]{:T(128)}) all-reduce(f32[]{:T(128)} %get-tuple-element.231, f32[]{:T(128)} %get-tuple-element.232), channel_id=1, replica_groups=mesh['grp_0'=2,'grp_1'=2,'mem_0'=2,'mem_1'=4,'mem_2'=4] {'mem_0'}, use_global_device_ids=true, to_apply=%region_13.0 | all-reduce | flops 2 | bytes 16 | tf_op jit(solution)/shard_map/pmax | solution.py:17
  19.3 11.1 %all-reduce.13 = (f32[]{:T(128)}, f32[]{:T(128)}) all-reduce(f32[]{:T(128)} %get-tuple-element.229, f32[]{:T(128)} %get-tuple-element.230), channel_id=1, replica_groups=mesh['grp_0'=2,'grp_1'=2,'mem_0'=2,'mem_1'=4,'mem_2'=4] {'mem_1'}, use_global_device_ids=true, to_apply=%region_14.0 | all-reduce | flops 2 | bytes 16 | tf_op jit(solution)/shard_map/pmax | solution.py:17
  30.4 11.4 %all-reduce.12 = (f32[]{:T(128)}, f32[]{:T(128)}) all-reduce(f32[]{:T(128)} %get-tuple-element.221, f32[]{:T(128)} %get-tuple-element.222), channel_id=1, replica_groups=mesh['grp_0'=2,'grp_1'=2,'mem_0'=2,'mem_1'=4,'mem_2'=4] {'mem_2'}, use_global_device_ids=true, to_apply=%region_15.0 | all-reduce | flops 2 | bytes 16 | tf_op jit(solution)/shard_map/pmax | solution.py:17
  50.3 5.5 %all-to-all-done = f32[4,65,256]{2,1,0:T(8,128)S(1)} async-done(((f32[4,65,256]{2,1,0:T(8,128)}), f32[4,65,256]{2,1,0:T(8,128)S(1)}, u32[]{:S(2)}, u32[]{:S(2)}) %all-to-all-start) | async-done | bytes 266272 | tf_op jit(solution)/shard_map/all_to_all | solution.py:35
  57.4 5.8 %all-to-all-start.1 = ((f32[32,65,256]{2,1,0:T(8,128)}), f32[32,65,256]{2,1,0:T(8,128)S(1)}, u32[]{:S(2)}, u32[]{:S(2)}) async-start(f32[32,65,256]{2,1,0:T(8,128)} %broadcast_in_dim.49), calls=%async_computation.1 | async-start | bytes 4718592 | tf_op jit(solution)/shard_map/all_to_all | solution.py:35
  63.5 31.0 %all-to-all-done.1 = f32[32,65,256]{2,1,0:T(8,128)S(1)} async-done(((f32[32,65,256]{2,1,0:T(8,128)}), f32[32,65,256]{2,1,0:T(8,128)S(1)}, u32[]{:S(2)}, u32[]{:S(2)}) %all-to-all-start.1) | async-done | bytes 2129952 | tf_op jit(solution)/shard_map/all_to_all | solution.py:35
  95.2 82.6 %while.20 = (s32[]{:T(128)}, f32[8192]{0:T(1024)S(1)}, f32[8192]{0:T(1024)S(1)}, f32[1024]{0:T(1024)S(1)}, f32[1024]{0:T(1024)S(1)}, /*index=5*/f32[65,1024]{1,0...) while((s32[]{:T(128)}, f32[8192]{0:T(1024)S(1)}, ...), condition=%wide.region_7.0_spmd.clone, body=%wide.region_1.0_spmd.clone.sunk | while | flops 818995456 | bytes 11102434 | solution.py:95
  95.3 6.0 %subtract_reduce_fusion.3 = (f32[128]{0:T(128)S(1)}, f32[8192]{0:T(1024)S(1)}, f32[8192,128]{0,1:T(8,128)}) fusion(f32[8192]{0:T(1024)S(1)} %bitcast.51, f32[128]{0:T(128)S(1)} %dynamic-slice_bitcast_fusion.2, f32[64,8192]{1,0:T(8,128)S(1)} %get-tuple-element.350, f32[65,1024]{1,0:T(8,128)S(1)} %get-tuple-element.348, s32[]{:T(128)S(6)} %select_n.21, ...), kind=kOutput, calls=%fused_computation.5.clone.1 | convolution fusion | flops 812638080 | bytes 6424068 | tf_op jit(solution)/shard_map/while/body/eval_jaxpr/dot_general | solution.py:70
  101.5 3.8 %exponential_reduce_fusion.5 = (f32[128]{0:T(128)S(1)}, f32[8192]{0:T(1024)S(1)}) fusion(f32[8192,128]{0,1:T(8,128)} %get-tuple-element.309, f32[128]{0:T(128)S(1)} %get-tuple-element.311, f32[8192]{0:T(1024)S(1)} %bitcast.52, f32[8192]{0:T(1024)S(1)} %select_maximum_fusion.2, f32[128]{0:T(128)S(1)} %dynamic-slice_bitcast_fusion.2), kind=kLoop, calls=%fused_computation.3.clone.1 | loop fusion | flops 6283136 | bytes 4294144 | tf_op jit(solution)/shard_map/while/body/eval_jaxpr/reduce_sum | solution.py:88
  105.6 6.0 %subtract_reduce_fusion.3 = (f32[128]{0:T(128)S(1)}, f32[8192]{0:T(1024)S(1)}, f32[8192,128]{0,1:T(8,128)}) fusion(f32[8192]{0:T(1024)S(1)} %bitcast.51, f32[128]{0:T(128)S(1)} %dynamic-slice_bitcast_fusion.2, f32[64,8192]{1,0:T(8,128)S(1)} %get-tuple-element.350, f32[65,1024]{1,0:T(8,128)S(1)} %get-tuple-element.348, s32[]{:T(128)S(6)} %select_n.21, ...), kind=kOutput, calls=%fused_computation.5.clone.1 | convolution fusion | flops 812638080 | bytes 6424068 | tf_op jit(solution)/shard_map/while/body/eval_jaxpr/dot_general | solution.py:70
  111.8 3.8 %exponential_reduce_fusion.5 = (f32[128]{0:T(128)S(1)}, f32[8192]{0:T(1024)S(1)}) fusion(f32[8192,128]{0,1:T(8,128)} %get-tuple-element.309, f32[128]{0:T(128)S(1)} %get-tuple-element.311, f32[8192]{0:T(1024)S(1)} %bitcast.52, f32[8192]{0:T(1024)S(1)} %select_maximum_fusion.2, f32[128]{0:T(128)S(1)} %dynamic-slice_bitcast_fusion.2), kind=kLoop, calls=%fused_computation.3.clone.1 | loop fusion | flops 6283136 | bytes 4294144 | tf_op jit(solution)/shard_map/while/body/eval_jaxpr/reduce_sum | solution.py:88
  115.9 6.0 %subtract_reduce_fusion.3 = (f32[128]{0:T(128)S(1)}, f32[8192]{0:T(1024)S(1)}, f32[8192,128]{0,1:T(8,128)}) fusion(f32[8192]{0:T(1024)S(1)} %bitcast.51, f32[128]{0:T(128)S(1)} %dynamic-slice_bitcast_fusion.2, f32[64,8192]{1,0:T(8,128)S(1)} %get-tuple-element.350, f32[65,1024]{1,0:T(8,128)S(1)} %get-tuple-element.348, s32[]{:T(128)S(6)} %select_n.21, ...), kind=kOutput, calls=%fused_computation.5.clone.1 | convolution fusion | flops 812638080 | bytes 6424068 | tf_op jit(solution)/shard_map/while/body/eval_jaxpr/dot_general | solution.py:70
  122.1 3.8 %exponential_reduce_fusion.5 = (f32[128]{0:T(128)S(1)}, f32[8192]{0:T(1024)S(1)}) fusion(f32[8192,128]{0,1:T(8,128)} %get-tuple-element.309, f32[128]{0:T(128)S(1)} %get-tuple-element.311, f32[8192]{0:T(1024)S(1)} %bitcast.52, f32[8192]{0:T(1024)S(1)} %select_maximum_fusion.2, f32[128]{0:T(128)S(1)} %dynamic-slice_bitcast_fusion.2), kind=kLoop, calls=%fused_computation.3.clone.1 | loop fusion | flops 6283136 | bytes 4294144 | tf_op jit(solution)/shard_map/while/body/eval_jaxpr/reduce_sum | solution.py:88
  126.3 6.0 %subtract_reduce_fusion.3 = (f32[128]{0:T(128)S(1)}, f32[8192]{0:T(1024)S(1)}, f32[8192,128]{0,1:T(8,128)}) fusion(f32[8192]{0:T(1024)S(1)} %bitcast.51, f32[128]{0:T(128)S(1)} %dynamic-slice_bitcast_fusion.2, f32[64,8192]{1,0:T(8,128)S(1)} %get-tuple-element.350, f32[65,1024]{1,0:T(8,128)S(1)} %get-tuple-element.348, s32[]{:T(128)S(6)} %select_n.21, ...), kind=kOutput, calls=%fused_computation.5.clone.1 | convolution fusion | flops 812638080 | bytes 6424068 | tf_op jit(solution)/shard_map/while/body/eval_jaxpr/dot_general | solution.py:70
  132.5 3.8 %exponential_reduce_fusion.5 = (f32[128]{0:T(128)S(1)}, f32[8192]{0:T(1024)S(1)}) fusion(f32[8192,128]{0,1:T(8,128)} %get-tuple-element.309, f32[128]{0:T(128)S(1)} %get-tuple-element.311, f32[8192]{0:T(1024)S(1)} %bitcast.52, f32[8192]{0:T(1024)S(1)} %select_maximum_fusion.2, f32[128]{0:T(128)S(1)} %dynamic-slice_bitcast_fusion.2), kind=kLoop, calls=%fused_computation.3.clone.1 | loop fusion | flops 6283136 | bytes 4294144 | tf_op jit(solution)/shard_map/while/body/eval_jaxpr/reduce_sum | solution.py:88
  136.6 6.0 %subtract_reduce_fusion.3 = (f32[128]{0:T(128)S(1)}, f32[8192]{0:T(1024)S(1)}, f32[8192,128]{0,1:T(8,128)}) fusion(f32[8192]{0:T(1024)S(1)} %bitcast.51, f32[128]{0:T(128)S(1)} %dynamic-slice_bitcast_fusion.2, f32[64,8192]{1,0:T(8,128)S(1)} %get-tuple-element.350, f32[65,1024]{1,0:T(8,128)S(1)} %get-tuple-element.348, s32[]{:T(128)S(6)} %select_n.21, ...), kind=kOutput, calls=%fused_computation.5.clone.1 | convolution fusion | flops 812638080 | bytes 6424068 | tf_op jit(solution)/shard_map/while/body/eval_jaxpr/dot_general | solution.py:70
  142.8 3.8 %exponential_reduce_fusion.5 = (f32[128]{0:T(128)S(1)}, f32[8192]{0:T(1024)S(1)}) fusion(f32[8192,128]{0,1:T(8,128)} %get-tuple-element.309, f32[128]{0:T(128)S(1)} %get-tuple-element.311, f32[8192]{0:T(1024)S(1)} %bitcast.52, f32[8192]{0:T(1024)S(1)} %select_maximum_fusion.2, f32[128]{0:T(128)S(1)} %dynamic-slice_bitcast_fusion.2), kind=kLoop, calls=%fused_computation.3.clone.1 | loop fusion | flops 6283136 | bytes 4294144 | tf_op jit(solution)/shard_map/while/body/eval_jaxpr/reduce_sum | solution.py:88
  146.9 6.0 %subtract_reduce_fusion.3 = (f32[128]{0:T(128)S(1)}, f32[8192]{0:T(1024)S(1)}, f32[8192,128]{0,1:T(8,128)}) fusion(f32[8192]{0:T(1024)S(1)} %bitcast.51, f32[128]{0:T(128)S(1)} %dynamic-slice_bitcast_fusion.2, f32[64,8192]{1,0:T(8,128)S(1)} %get-tuple-element.350, f32[65,1024]{1,0:T(8,128)S(1)} %get-tuple-element.348, s32[]{:T(128)S(6)} %select_n.21, ...), kind=kOutput, calls=%fused_computation.5.clone.1 | convolution fusion | flops 812638080 | bytes 6424068 | tf_op jit(solution)/shard_map/while/body/eval_jaxpr/dot_general | solution.py:70
  153.1 3.8 %exponential_reduce_fusion.5 = (f32[128]{0:T(128)S(1)}, f32[8192]{0:T(1024)S(1)}) fusion(f32[8192,128]{0,1:T(8,128)} %get-tuple-element.309, f32[128]{0:T(128)S(1)} %get-tuple-element.311, f32[8192]{0:T(1024)S(1)} %bitcast.52, f32[8192]{0:T(1024)S(1)} %select_maximum_fusion.2, f32[128]{0:T(128)S(1)} %dynamic-slice_bitcast_fusion.2), kind=kLoop, calls=%fused_computation.3.clone.1 | loop fusion | flops 6283136 | bytes 4294144 | tf_op jit(solution)/shard_map/while/body/eval_jaxpr/reduce_sum | solution.py:88
  157.3 6.0 %subtract_reduce_fusion.3 = (f32[128]{0:T(128)S(1)}, f32[8192]{0:T(1024)S(1)}, f32[8192,128]{0,1:T(8,128)}) fusion(f32[8192]{0:T(1024)S(1)} %bitcast.51, f32[128]{0:T(128)S(1)} %dynamic-slice_bitcast_fusion.2, f32[64,8192]{1,0:T(8,128)S(1)} %get-tuple-element.350, f32[65,1024]{1,0:T(8,128)S(1)} %get-tuple-element.348, s32[]{:T(128)S(6)} %select_n.21, ...), kind=kOutput, calls=%fused_computation.5.clone.1 | convolution fusion | flops 812638080 | bytes 6424068 | tf_op jit(solution)/shard_map/while/body/eval_jaxpr/dot_general | solution.py:70
  163.4 3.8 %exponential_reduce_fusion.5 = (f32[128]{0:T(128)S(1)}, f32[8192]{0:T(1024)S(1)}) fusion(f32[8192,128]{0,1:T(8,128)} %get-tuple-element.309, f32[128]{0:T(128)S(1)} %get-tuple-element.311, f32[8192]{0:T(1024)S(1)} %bitcast.52, f32[8192]{0:T(1024)S(1)} %select_maximum_fusion.2, f32[128]{0:T(128)S(1)} %dynamic-slice_bitcast_fusion.2), kind=kLoop, calls=%fused_computation.3.clone.1 | loop fusion | flops 6283136 | bytes 4294144 | tf_op jit(solution)/shard_map/while/body/eval_jaxpr/reduce_sum | solution.py:88
  167.6 6.0 %subtract_reduce_fusion.3 = (f32[128]{0:T(128)S(1)}, f32[8192]{0:T(1024)S(1)}, f32[8192,128]{0,1:T(8,128)}) fusion(f32[8192]{0:T(1024)S(1)} %bitcast.51, f32[128]{0:T(128)S(1)} %dynamic-slice_bitcast_fusion.2, f32[64,8192]{1,0:T(8,128)S(1)} %get-tuple-element.350, f32[65,1024]{1,0:T(8,128)S(1)} %get-tuple-element.348, s32[]{:T(128)S(6)} %select_n.21, ...), kind=kOutput, calls=%fused_computation.5.clone.1 | convolution fusion | flops 812638080 | bytes 6424068 | tf_op jit(solution)/shard_map/while/body/eval_jaxpr/dot_general | solution.py:70
  177.9 6.2 %all_to_all.40 = f32[4,1,1024]{2,1,0:T(1,128)S(1)} all-to-all(f32[4,1,1024]{2,1,0:T(1,128)S(1)} %broadcast_in_dim.51), channel_id=1, replica_groups=mesh['grp_0'=2,'grp_1'=2,'mem_0'=2,'mem_1'=4,'mem_2'=4] {'grp_0','grp_1'}, dimensions={0} | all-to-all | bytes 32768 | tf_op jit(solution)/shard_map/all_to_all | solution.py:35
  184.1 6.1 %all_to_all.41 = f32[4,1,256]{2,1,0:T(1,128)S(1)} all-to-all(f32[4,1,256]{2,1,0:T(1,128)S(1)} %bitcast.57), channel_id=1, replica_groups=mesh['grp_0'=2,'grp_1'=2,'mem_0'=2,'mem_1'=4,'mem_2'=4] {'grp_0','grp_1'}, dimensions={0} | all-to-all | bytes 8192 | tf_op jit(solution)/shard_map/all_to_all | solution.py:54
  192.2 7.5 %all-to-all-start.2 = ((f32[32,1,8192]{2,1,0:T(1,128)}), f32[32,1,8192]{2,1,0:T(1,128)S(1)}, u32[]{:S(2)}, u32[]{:S(2)}) async-start(f32[32,1,8192]{2,1,0:T(1,128)} %broadcast_in_dim.50), calls=%async_computation.2 | async-start | bytes 2097152 | tf_op jit(solution)/shard_map/all_to_all | solution.py:35
  203.1 5.3 %all-reduce.16 = (f32[2]{0:T(128)S(1)}, f32[2]{0:T(128)S(1)}) all-reduce(f32[2]{0:T(128)S(1)} %dynamic-update-slice, f32[2]{0:T(128)S(1)} %dynamic-update-slice.5), channel_id=1, replica_groups=mesh['grp_0'=2,'grp_1'=2,'mem_0'=2,'mem_1'=4,'mem_2'=4] {'grp_0'}, use_global_device_ids=true, to_apply=%add | all-reduce | flops 4 | bytes 32
  220.1 6.4 %all-reduce.14 = (f32[2]{0:T(128)S(1)}, f32[2]{0:T(128)S(1)}) all-reduce(f32[2]{0:T(128)S(1)} %dynamic-update-slice.2, f32[2]{0:T(128)S(1)} %dynamic-update-slice.7), channel_id=1, replica_groups=mesh['grp_0'=2,'grp_1'=2,'mem_0'=2,'mem_1'=4,'mem_2'=4] {'mem_0'}, use_global_device_ids=true, to_apply=%add.2 | all-reduce | flops 4 | bytes 32
  231.2 13.5 %all-reduce.11 = (f32[4]{0:T(128)S(1)}, f32[4]{0:T(128)S(1)}) all-reduce(f32[4]{0:T(128)S(1)} %dynamic-update-slice.3, f32[4]{0:T(128)S(1)} %dynamic-update-slice.8), channel_id=1, replica_groups=mesh['grp_0'=2,'grp_1'=2,'mem_0'=2,'mem_1'=4,'mem_2'=4] {'mem_1'}, use_global_device_ids=true, to_apply=%add.3 | all-reduce | flops 8 | bytes 64
  249.3 10.2 %all-reduce.10 = (f32[4]{0:T(128)S(1)}, f32[4]{0:T(128)S(1)}) all-reduce(f32[4]{0:T(128)S(1)} %dynamic-update-slice.4, f32[4]{0:T(128)S(1)} %dynamic-update-slice.9), channel_id=1, replica_groups=mesh['grp_0'=2,'grp_1'=2,'mem_0'=2,'mem_1'=4,'mem_2'=4] {'mem_2'}, use_global_device_ids=true, to_apply=%add.4 | all-reduce | flops 8 | bytes 64
  264.8 5.8 %all-to-all-start.3 = ((f32[32,1,256]{2,1,0:T(1,128)}), f32[32,1,256]{2,1,0:T(1,128)S(1)}, u32[]{:S(2)}, u32[]{:S(2)}) async-start(f32[32,1,256]{2,1,0:T(1,128)} %bitcast.5), calls=%async_computation.3 | async-start | bytes 65536 | tf_op jit(solution)/shard_map/all_to_all | solution.py:54
  271.2 9.2 %all-to-all-done.3 = f32[32,1,256]{2,1,0:T(1,128)S(1)} async-done(((f32[32,1,256]{2,1,0:T(1,128)}), f32[32,1,256]{2,1,0:T(1,128)S(1)}, u32[]{:S(2)}, u32[]{:S(2)}) %all-to-all-start.3) | async-done | bytes 32800 | tf_op jit(solution)/shard_map/all_to_all | solution.py:54
  (163 shorter events, 54.5 us)
Async XLA Ops:
  46.0 9.8 %all-to-all-start = ((f32[4,65,256]{2,1,0:T(8,128)}), f32[4,65,256]{2,1,0:T(8,128)S(1)}, u32[]{:S(2)}, u32[]{:S(2)}) async-start(f32[4,65,256]{2,1,0:T(8,128)} %broadcast_in_dim.47), calls=%async_computation | async-start | bytes 589824 | tf_op jit(solution)/shard_map/all_to_all | solution.py:35
  57.4 37.1 %all-to-all-start.1 = ((f32[32,65,256]{2,1,0:T(8,128)}), f32[32,65,256]{2,1,0:T(8,128)S(1)}, u32[]{:S(2)}, u32[]{:S(2)}) async-start(f32[32,65,256]{2,1,0:T(8,128)} %broadcast_in_dim.49), calls=%async_computation.1 | async-start | bytes 4718592 | tf_op jit(solution)/shard_map/all_to_all | solution.py:35
  95.2 104.5 %copy-start.6 = (u32[128]{0:T(128)S(1)}, u32[128]{0:T(128)}, u32[]{:S(2)}) copy-start(u32[128]{0:T(128)} %constant.108) | copy-start | bytes 1540
  95.2 113.2 %copy-start.5 = (u32[128]{0:T(128)S(1)}, u32[128]{0:T(128)}, u32[]{:S(2)}) copy-start(u32[128]{0:T(128)} %constant.113) | copy-start | bytes 1540
  95.2 120.3 %copy-start.4 = (u32[128]{0:T(128)S(1)}, u32[128]{0:T(128)}, u32[]{:S(2)}) copy-start(u32[128]{0:T(128)} %constant.118) | copy-start | bytes 1540
  95.2 131.3 %copy-start.3 = (u32[128]{0:T(128)S(1)}, u32[128]{0:T(128)}, u32[]{:S(2)}) copy-start(u32[128]{0:T(128)} %constant.123) | copy-start | bytes 1540
  95.2 149.5 %copy-start.2 = (u32[128]{0:T(128)S(1)}, u32[128]{0:T(128)}, u32[]{:S(2)}) copy-start(u32[128]{0:T(128)} %constant.128) | copy-start | bytes 1540
  177.8 92.7 %copy-start = (f32[256]{0:T(256)S(1)}, f32[256]{0:T(256)}, u32[]{:S(2)}) copy-start(f32[256]{0:T(256)} %param.11) | copy-start | bytes 3076
  177.9 102.6 %copy-start.1 = (f32[256]{0:T(256)S(1)}, f32[256]{0:T(256)}, u32[]{:S(2)}) copy-start(f32[256]{0:T(256)} %param.10) | copy-start | bytes 3076
  192.2 71.2 %all-to-all-start.2 = ((f32[32,1,8192]{2,1,0:T(1,128)}), f32[32,1,8192]{2,1,0:T(1,128)S(1)}, u32[]{:S(2)}, u32[]{:S(2)}) async-start(f32[32,1,8192]{2,1,0:T(1,128)} %broadcast_in_dim.50), calls=%async_computation.2 | async-start | bytes 2097152 | tf_op jit(solution)/shard_map/all_to_all | solution.py:35
  264.8 15.6 %all-to-all-start.3 = ((f32[32,1,256]{2,1,0:T(1,128)}), f32[32,1,256]{2,1,0:T(1,128)S(1)}, u32[]{:S(2)}, u32[]{:S(2)}) async-start(f32[32,1,256]{2,1,0:T(1,128)} %bitcast.5), calls=%async_computation.3 | async-start | bytes 65536 | tf_op jit(solution)/shard_map/all_to_all | solution.py:54
